TPU v7x, 128 devices: a whole 4x4x4 slice. The times are simulated.
128 devices in a mesh: row: 8 (over y, core), col: 16 (over x, z).
Axes of the slice: x: 4, y: 4, z: 4, core: 2. Of those that a mesh axis runs over, the one named last changes fastest.
Arguments:
- atom_rows: bfloat16 [48, 8192, 128], P(None, ('row', 'col')), may hold values from -48 to 48
- pair_rep: bfloat16 [1024, 1024, 128], P('row', 'col'), may hold values from -6 to 6
- query_gate_weight: bfloat16 [128, 256], replicated, may hold values from -0.5 to 0.5
- key_value_weight: bfloat16 [128, 256], replicated, may hold values from -0.5 to 0.5
- output_weight: bfloat16 [128, 128], replicated, may hold values from -2 to 2
- pair_weight: float32 [128, 4], replicated, may hold values from -0.5 to 0.5
- counts: int32 [128, 8], replicated, may hold values from 1 to 24, 64 in all within a row
- token_mask: int32 [1024], replicated, may hold values 0 or 1
- cotangent: bfloat16 [48, 8192, 128], P(None, ('row', 'col')), may hold values from -6 to 6
Outputs:
- updated_atoms: bfloat16 [48, 8192, 128], P(None, ('row', 'col'))
- atom_grad: bfloat16 [48, 8192, 128], P(None, ('row', 'col'))
- pair_grad: bfloat16 [1024, 1024, 128], P('row', 'col')
- pair_weight_grad: float32 [128, 4], replicated
Inputs may be any that keep to these rules, and one draw needn't show every extreme that they name: Each row of counts sums to 64, so the atoms of one aligned block of 8 tokens are one aligned block of 64 atoms; the largest entry of each row is 24.
All inputs are finite; a program needn't handle non-finite values.
Results may differ from a plain program's by a relative error of at most 0.028.
Values may be sent and summed in bfloat16 or wider, within the bound.
A program may use at most 128 MiB of HBM per device.

v0:
```python
import functools
import math

import jax
import jax.numpy as jnp
from jax import lax
from jax.experimental import pallas as pl
from jax.experimental.pallas import tpu as pltpu
from jax.sharding import PartitionSpec as P

BLOCK = 64
TOK = 8
HEADS = 4
WIN = 32
KEYS = 128
HALO = 48
CH = 128
EXT = BLOCK + 2 * HALO
LANES = 2 * HEADS * WIN
EPS = 1e-05
MASKED = -1000000000.0
SCALE = 1.0 / math.sqrt(CH // HEADS)
STEP = 4
AHEAD = 3
LAG = 4
DELAY = 4
HALF = 2

F32 = jnp.float32
BF16 = jnp.bfloat16
HI = lax.Precision.HIGHEST
MESH = pl.DeviceIdType.MESH


def nn(a, b, precision=None):
    return lax.dot_general(a, b, (((1,), (0,)), ((), ())), precision=precision, preferred_element_type=F32)


def nt(a, b, precision=None):
    return lax.dot_general(a, b, (((1,), (1,)), ((), ())), precision=precision, preferred_element_type=F32)


def tn(a, b, precision=None):
    return lax.dot_general(a, b, (((0,), (0,)), ((), ())), precision=precision, preferred_element_type=F32)


def iota(shape, dim):
    return lax.broadcasted_iota(jnp.int32, shape, dim)


def normalize(values):
    centered = values - jnp.mean(values, axis=1, keepdims=True)
    rstd = lax.rsqrt(jnp.mean(centered * centered, axis=1, keepdims=True) + EPS)
    return centered * rstd, rstd


def totals_of(counts, group):
    running, total = [], 0
    for j in range(TOK):
        total = total + counts[j, group]
        running.append(total)
    return running


def main_kernel(
    rows, cols, samples,
    counts_hbm, mask_hbm, x_hbm, pair_hbm, wqg_hbm, wkv_hbm, wo_hbm, pw_hbm, dy_hbm,
    upd_v, grad_v, pair_out, wgrad_out,
    counts, mask, wqg_ref, wkv_ref, wo_ref, pwt_v, pw_v,
    x_v, dy_v, lo_v, hi_v, glo_v, ghi_v, gprev_v, gnext_v, center_v,
    band_v, bandgrad_v, piece_v, bt_v, dbt_v, kv_v, dkv_v, q_v, gate_v, dgated_v, gated_v, dgate_v, dq_v,
    datt_v, prob_v, dscore_v, logit_v, dprob_v,
    red_a, red_b, part_a, part_b,
    in_sem, lo_send, hi_send, lo_recv, hi_recv, glo_send, ghi_send, gp_recv, gn_recv,
    band_send, band_recv, piece_send, piece_recv, a_send, a_recv, b_send, b_recv,
):
    chunks = samples // STEP
    blocks = rows * cols
    row = lax.axis_index("row")
    col = lax.axis_index("col")
    me = row * cols + col
    has_prev = me > 0
    has_next = me < blocks - 1
    before = jnp.maximum(me - 1, 0)
    after = jnp.minimum(me + 1, blocks - 1)
    prev_id = (before // cols, before % cols)
    next_id = (after // cols, after % cols)

    barrier = pltpu.get_barrier_semaphore()

    @pl.loop(1, cols)
    def _(d):
        pl.semaphore_signal(barrier, inc=1, device_id=(row, lax.rem(col + d, cols)), device_id_type=MESH)

    @pl.loop(1, rows)
    def _(d):
        pl.semaphore_signal(barrier, inc=1, device_id=(lax.rem(row + d, rows), col), device_id_type=MESH)

    far_next = jnp.logical_and(col == cols - 1, has_next)
    far_prev = jnp.logical_and(col == 0, has_prev)

    @pl.when(far_next)
    def _():
        pl.semaphore_signal(barrier, inc=1, device_id=next_id, device_id_type=MESH)

    @pl.when(far_prev)
    def _():
        pl.semaphore_signal(barrier, inc=1, device_id=prev_id, device_id_type=MESH)

    small_in = [
        pltpu.make_async_copy(src, dst, in_sem.at[n])
        for n, (src, dst) in enumerate([(counts_hbm, counts), (mask_hbm, mask), (pw_hbm, pwt_v)])
    ]
    large_in = [
        pltpu.make_async_copy(src, dst, in_sem.at[3 + n])
        for n, (src, dst) in enumerate(
            [(wkv_hbm, wkv_ref), (wqg_hbm, wqg_ref), (wo_hbm, wo_ref), (x_hbm, x_v), (dy_hbm, dy_v)])
    ]
    for copy in small_in + large_in:
        copy.start()

    @pl.when(jnp.logical_not(has_prev))
    def _():
        lo_v[...] = jnp.zeros_like(lo_v)
        gprev_v[...] = jnp.zeros_like(gprev_v)
        band_v[:, :TOK] = jnp.zeros((TOK, TOK, CH), BF16)

    @pl.when(jnp.logical_not(has_next))
    def _():
        hi_v[...] = jnp.zeros_like(hi_v)
        gnext_v[...] = jnp.zeros_like(gnext_v)
        band_v[:, 2 * TOK :] = jnp.zeros((TOK, TOK, CH), BF16)

    for copy in small_in:
        copy.wait()

    g_prev = jnp.maximum(me - 1, 0)
    g_next = jnp.minimum(me + 1, blocks - 1)
    run_prev, run_own, run_next = totals_of(counts, g_prev), totals_of(counts, me), totals_of(counts, g_next)
    atom = iota((EXT, 32), 0)
    is_lo, is_hi = atom < HALO, atom >= HALO + BLOCK
    local = jnp.where(is_lo, atom + (BLOCK - HALO), jnp.where(is_hi, atom - (HALO + BLOCK), atom - HALO))
    token = jnp.where(is_lo, 0, jnp.where(is_hi, 2 * TOK, TOK))
    for j in range(TOK):
        limit = jnp.where(is_lo, run_prev[j], jnp.where(is_hi, run_next[j], run_own[j]))
        token = token + (limit <= local).astype(jnp.int32)
    key_hot32 = (token == iota((EXT, 32), 1)).astype(F32)
    key_hot = key_hot32.astype(BF16)

    lane = iota((TOK, LANES), 1)
    query = (lane // KEYS) * WIN + lane % WIN
    query_token = jnp.zeros((TOK, LANES), jnp.int32)
    for j in range(TOK):
        query_token = query_token + (run_own[j] <= query).astype(jnp.int32)

    slot_row = iota((32, LANES), 0)
    mask_rows = jnp.zeros((32, LANES), F32)
    for u in range(3 * TOK):
        where_to = me * TOK + u - TOK
        bit = mask[jnp.clip(where_to, 0, blocks * TOK - 1)]
        bit = jnp.where(jnp.logical_and(where_to >= 0, where_to < blocks * TOK), bit, 0)
        mask_rows = jnp.where(slot_row == u, bit.astype(F32), mask_rows)
    valid = nn(key_hot, mask_rows.astype(BF16))

    pl.semaphore_wait(
        barrier, (cols - 1) + (rows - 1) + far_next.astype(jnp.int32) + far_prev.astype(jnp.int32)
    )

    def to_next(i):
        return pltpu.make_async_remote_copy(
            src_ref=x_hbm.at[pl.ds(i * STEP, STEP), pl.ds(BLOCK - HALO, HALO)],
            dst_ref=lo_v.at[pl.ds(i * STEP, STEP)],
            send_sem=lo_send.at[i], recv_sem=lo_recv.at[i],
            device_id=next_id, device_id_type=MESH)

    def to_prev(i):
        return pltpu.make_async_remote_copy(
            src_ref=x_hbm.at[pl.ds(i * STEP, STEP), pl.ds(0, HALO)],
            dst_ref=hi_v.at[pl.ds(i * STEP, STEP)],
            send_sem=hi_send.at[i], recv_sem=hi_recv.at[i],
            device_id=prev_id, device_id_type=MESH)

    def grad_to_prev(i):
        return pltpu.make_async_remote_copy(
            src_ref=glo_v.at[pl.ds(i * STEP, STEP)],
            dst_ref=gnext_v.at[pl.ds(i * STEP, STEP)],
            send_sem=glo_send.at[i], recv_sem=gn_recv.at[i],
            device_id=prev_id, device_id_type=MESH)

    def grad_to_next(i):
        return pltpu.make_async_remote_copy(
            src_ref=ghi_v.at[pl.ds(i * STEP, STEP)],
            dst_ref=gprev_v.at[pl.ds(i * STEP, STEP)],
            send_sem=ghi_send.at[i], recv_sem=gp_recv.at[i],
            device_id=next_id, device_id_type=MESH)

    delta = rows * col - cols * row

    def inside(j):
        return jnp.logical_and(j >= 0, j < cols)

    def clamped(j):
        return jnp.clip(j, 0, cols - 1)

    def band_refs(d, j, wide, first):
        k = d - 1 + first
        return (
            pair_hbm.at[pl.ds(j * TOK, TOK), pl.ds(pl.multiple_of(k * TOK, TOK), wide * TOK)],
            band_v.at[:, pl.ds(first * TOK, wide * TOK)])

    def band_copy(d, j, wide, first):
        src, dst = band_refs(d, j, wide, first)
        return pltpu.make_async_remote_copy(
            src_ref=src, dst_ref=dst,
            send_sem=band_send.at[d + 1], recv_sem=band_recv.at[0 if wide > 1 else 1],
            device_id=(row, j), device_id_type=MESH)

    def band_local(d, j, wide, first):
        src, dst = band_refs(d, j, wide, first)
        return pltpu.make_async_copy(src, dst, band_send.at[d + 1])

    def send_band(d, wide, first):
        j = delta + d

        @pl.when(jnp.logical_and(inside(j), j != col))
        def _():
            band_copy(d, clamped(j), wide, first).start()

        @pl.when(jnp.logical_and(inside(j), j == col))
        def _():
            band_local(d, clamped(j), wide, first).start()

    def band_sent(d, wide, first):
        j = delta + d

        @pl.when(jnp.logical_and(inside(j), j != col))
        def _():
            band_copy(d, clamped(j), wide, first).wait_send()

    def all_readers(act):
        @pl.loop(1, rows - 1)
        def _(d):
            act(d, 3, 0)

        act(0, 2, 1)
        act(rows - 1, 2, 0)
        act(-1, 1, 2)
        act(rows, 1, 0)

    owner = me // rows
    mine = me % rows
    side_low = jnp.logical_and(mine == 0, has_prev)
    side_high = jnp.logical_and(mine == rows - 1, has_next)

    def receive_band(cond, source, d, wide, first):
        @pl.when(jnp.logical_and(cond, source != col))
        def _():
            band_copy(d, col, wide, first).wait_recv()

        @pl.when(jnp.logical_and(cond, source == col))
        def _():
            band_local(d, col, wide, first).wait()

    def piece_copy(target, d, wide, first):
        at = pl.ds(first * TOK, wide * TOK)
        return pltpu.make_async_remote_copy(
            src_ref=bandgrad_v.at[:, at], dst_ref=piece_v.at[d + 1, :, at],
            send_sem=piece_send.at[0 if wide > 1 else 1], recv_sem=piece_recv.at[d + 1],
            device_id=(row, target), device_id_type=MESH)

    def to_owners(act):
        act(jnp.logical_and(mine > 0, mine < rows - 1), owner, mine, 3, 0)
        act(mine == 0, owner, 0, 2, 1)
        act(mine == rows - 1, owner, rows - 1, 2, 0)
        act(side_high, owner + 1, -1, 1, 2)
        act(side_low, owner - 1, rows, 1, 0)

    def send_rows(i):
        @pl.when(has_next)
        def _():
            to_next(i).start()

        @pl.when(has_prev)
        def _():
            to_prev(i).start()

    send_rows(0)
    all_readers(send_band)

    @pl.loop(1, AHEAD)
    def _(i):
        send_rows(i)

    to_owners(receive_band)

    def band_normed():
        return normalize(
            jnp.concatenate(
                [band_v[t, s * TOK : (s + 1) * TOK].astype(F32) for s in range(3) for t in range(TOK)], axis=0))

    pw_v[...] = jnp.concatenate([pwt_v[...], jnp.zeros((8 - HEADS, CH), F32)], axis=0).T
    head_lane = (iota((CH, LANES), 1) % KEYS) // WIN
    spread_weight = jnp.zeros((CH, LANES), F32)
    for h in range(HEADS):
        spread_weight = jnp.where(head_lane == h, pw_v[:, h : h + 1], spread_weight)
    normed, _ = band_normed()
    projected = nn(normed, spread_weight, HI)
    table = []
    for s in range(3):
        part = jnp.zeros((TOK, LANES), F32)
        for t in range(TOK):
            at = (s * TOK + t) * TOK
            part = jnp.where(query_token == t, projected[at : at + TOK], part)
        table.append(part)
    table = jnp.concatenate(table, axis=0)
    table = jnp.concatenate([table, jnp.zeros((8, LANES), F32)], axis=0).astype(BF16)
    bias = jnp.where(valid > 0.5, nn(key_hot, table), nn(key_hot, table) + MASKED)
    for w in range(2):
        bt_v[w] = bias[w * WIN : w * WIN + KEYS, w * KEYS : (w + 1) * KEYS]
    dbt_v[...] = jnp.zeros_like(dbt_v)
    pair_out[...] = jnp.zeros_like(pair_out)

    head_of = iota((WIN, CH), 1) // WIN
    head_mask = [(head_of == h).astype(BF16) for h in range(HEADS)]

    def expand(a):
        return jnp.concatenate(
            [a[w * WIN : (w + 1) * WIN] * head_mask[h] for w in range(2) for h in range(HEADS)], axis=0)

    def fold(a):
        out = a[:WIN]
        for h in range(1, HEADS):
            out = jnp.where(head_of == h, a[h * WIN : (h + 1) * WIN], out)
        return out

    gap = jnp.zeros((WIN, KEYS), BF16)

    def both(a0, a1):
        return jnp.concatenate(
            [jnp.concatenate([a0, gap], axis=0), jnp.concatenate([gap, a1], axis=0)], axis=1)

    for copy in large_in:
        copy.wait()

    def finish(i):
        @pl.when(has_next)
        def _():
            grad_to_prev(i).wait_recv()

        @pl.when(has_prev)
        def _():
            grad_to_next(i).wait_recv()

        part = pl.ds(i * STEP, STEP)
        from_prev = gprev_v[part].astype(F32)
        from_next = gnext_v[part].astype(F32)
        cut = BLOCK - HALO
        grad_v[part, 0:cut] = (center_v[part, 0:cut] + from_prev[:, :cut]).astype(BF16)
        grad_v[part, cut:HALO] = (
            center_v[part, cut:HALO] + from_prev[:, cut:] + from_next[:, : HALO - cut]).astype(BF16)
        grad_v[part, HALO:BLOCK] = (center_v[part, HALO:BLOCK] + from_next[:, HALO - cut :]).astype(BF16)

    def first_pass(i):
        @pl.when(i + AHEAD < chunks)
        def _():
            send_rows(i + AHEAD)

        part = pl.ds(i * STEP, STEP)
        x3 = x_v[part]
        x = x3.reshape(STEP * BLOCK, CH)
        dy = dy_v[part].reshape(STEP * BLOCK, CH)
        query_gate = nn(x, wqg_ref[...])
        q_v[part] = query_gate[:, :CH].astype(BF16).reshape(STEP, BLOCK, CH)
        gate_v[...] = jax.nn.sigmoid(query_gate[:, CH:]).reshape(STEP, BLOCK, CH)
        dgated_v[...] = nt(dy, wo_ref[...]).astype(BF16).reshape(STEP, BLOCK, CH)
        kv_v[part, HALO : HALO + BLOCK] = nn(x, wkv_ref[...]).astype(BF16).reshape(STEP, BLOCK, 2 * CH)

        @pl.when(has_prev)
        def _():
            to_next(i).wait_recv()

        @pl.when(has_next)
        def _():
            to_prev(i).wait_recv()

        lo = lo_v[part].reshape(STEP * HALO, CH)
        hi = hi_v[part].reshape(STEP * HALO, CH)
        kv_v[part, :HALO] = nn(lo, wkv_ref[...]).astype(BF16).reshape(STEP, HALO, 2 * CH)
        kv_v[part, HALO + BLOCK :] = nn(hi, wkv_ref[...]).astype(BF16).reshape(STEP, HALO, 2 * CH)

        for s in range(STEP):
            at = i * STEP + s
            datt = (dgated_v[s].astype(F32) * gate_v[s]).astype(BF16)
            datt_v[at] = datt
            logit_v[s] = nt(kv_v[at, :, :CH], expand(q_v[at]))
            dprob_v[s] = nt(kv_v[at, :, CH:], expand(datt))
        for w in range(2):
            ks = slice(w * WIN, w * WIN + KEYS)
            ls = slice(w * KEYS, (w + 1) * KEYS)
            for s in range(STEP):
                at = i * STEP + s
                score = logit_v[s, ks, ls] * SCALE + bt_v[w]
                e = jnp.exp(score - jnp.max(score, axis=0, keepdims=True))
                p = e * (1.0 / jnp.sum(e, axis=0, keepdims=True))
                t = dprob_v[s, ks, ls] * p
                ds = t - p * jnp.sum(t, axis=0, keepdims=True)
                dbt_v[w] += ds
                prob_v[at, w] = p.astype(BF16)
                dscore_v[at, w] = ds.astype(BF16)
        for s in range(STEP):
            at = i * STEP + s
            gate = gate_v[s]
            mixed = [fold(tn(prob_v[at, w], kv_v[at, w * WIN : w * WIN + KEYS, CH:])) for w in range(2)]
            attended = jnp.concatenate(mixed, axis=0)
            gated_v[s] = (attended * gate).astype(BF16)
            dgate_v[at] = (dgated_v[s].astype(F32) * attended * (gate * (1.0 - gate))).astype(BF16)

        out = x.astype(F32) + nn(gated_v[...].reshape(STEP * BLOCK, CH), wo_ref[...])
        upd_v[part] = out.astype(BF16).reshape(STEP, BLOCK, CH)

    def second_pass(i):
        part = pl.ds(i * STEP, STEP)
        for s in range(STEP):
            at = i * STEP + s
            dkv_v[s, :, :CH] = (nn(both(dscore_v[at, 0], dscore_v[at, 1]), expand(q_v[at])) * SCALE).astype(BF16)
            dkv_v[s, :, CH:] = nn(both(prob_v[at, 0], prob_v[at, 1]), expand(datt_v[at])).astype(BF16)

        glo = nt(dkv_v[:, :HALO].reshape(STEP * HALO, 2 * CH), wkv_ref[...])
        glo_v[part] = glo.astype(BF16).reshape(STEP, HALO, CH)
        ghi = nt(dkv_v[:, HALO + BLOCK :].reshape(STEP * HALO, 2 * CH), wkv_ref[...])
        ghi_v[part] = ghi.astype(BF16).reshape(STEP, HALO, CH)

        @pl.when(has_prev)
        def _():
            grad_to_prev(i).start()

        @pl.when(has_next)
        def _():
            grad_to_next(i).start()

        for s in range(STEP):
            at = i * STEP + s
            for w in range(2):
                dq = fold(tn(dscore_v[at, w], kv_v[at, w * WIN : w * WIN + KEYS, :CH]))
                dq_v[s, w * WIN : (w + 1) * WIN] = (dq * SCALE).astype(BF16)
        dquery = dq_v[...].reshape(STEP * BLOCK, CH)
        dgate = dgate_v[part].reshape(STEP * BLOCK, CH)
        own = nt(dkv_v[:, HALO : HALO + BLOCK].reshape(STEP * BLOCK, 2 * CH), wkv_ref[...])
        own = own + nt(jnp.concatenate([dquery, dgate], axis=1), wqg_ref[...])
        own = own + dy_v[part].reshape(STEP * BLOCK, CH).astype(F32)
        center_v[part] = own.reshape(STEP, BLOCK, CH)

        @pl.when(i >= LAG)
        def _():
            finish(i - LAG)

    def a_copy(peer, slot):
        return pltpu.make_async_remote_copy(
            src_ref=part_a, dst_ref=red_a.at[slot],
            send_sem=a_send.at[peer], recv_sem=a_recv.at[slot],
            device_id=(row, peer), device_id_type=MESH)

    def b_copy(peer, slot):
        return pltpu.make_async_remote_copy(
            src_ref=part_b, dst_ref=red_b.at[slot],
            send_sem=b_send.at[peer], recv_sem=b_recv.at[slot],
            device_id=(peer, col), device_id_type=MESH)

    @pl.loop(0, chunks)
    def _(i):
        first_pass(i)

        @pl.when(i >= DELAY)
        def _():
            second_pass(i - DELAY)

    gap32 = jnp.zeros((WIN, KEYS), F32)
    dbias = jnp.concatenate(
        [jnp.concatenate([dbt_v[0], gap32], axis=0), jnp.concatenate([gap32, dbt_v[1]], axis=0)], axis=1)
    dtable = tn(key_hot32, dbias, HI)[: 3 * TOK]
    by_token = jnp.concatenate(
        [
            jnp.where(query_token == t, dtable[s * TOK : (s + 1) * TOK], 0.0)
            for s in range(3) for t in range(TOK)
        ], axis=0)
    head_row = (iota((8, LANES), 1) % KEYS) // WIN
    to_head = (head_row == iota((8, LANES), 0)).astype(F32)
    dbias_rows = nt(to_head, by_token, HI).astype(BF16).astype(F32)
    normed, rstd = band_normed()
    part_a[...] = nn(dbias_rows, normed, HI)
    red_a[col] = part_a[...]

    @pl.loop(1, cols)
    def _(d):
        a_copy(lax.rem(col + d, cols), col).start()

    weight = jnp.concatenate([pwt_v[...], jnp.zeros((8 - HEADS, CH), F32)], axis=0)
    dnormed = tn(dbias_rows, weight, HI)
    dvalues = rstd * (
        dnormed - jnp.mean(dnormed, axis=1, keepdims=True)
        - normed * jnp.mean(dnormed * normed, axis=1, keepdims=True))
    for s in range(3):
        for t in range(TOK):
            at = (s * TOK + t) * TOK
            bandgrad_v[t, s * TOK : (s + 1) * TOK] = dvalues[at : at + TOK].astype(BF16)

    def send_piece(cond, target, d, wide, first):
        @pl.when(jnp.logical_and(cond, target != col))
        def _():
            piece_copy(target, d, wide, first).start()

        @pl.when(jnp.logical_and(cond, target == col))
        def _():
            piece_v[d + 1] = bandgrad_v[...]

    to_owners(send_piece)

    @pl.loop(chunks - DELAY, chunks - DELAY + HALF)
    def _(i):
        second_pass(i)

    @pl.loop(1, cols)
    def _(d):
        source = lax.rem(col + d, cols)
        a_copy(source, source).wait_recv()

    total = red_a[0]
    for j in range(1, cols):
        total = total + red_a[j]
    part_b[...] = total
    red_b[row] = total

    @pl.loop(1, rows)
    def _(d):
        b_copy(lax.rem(row + d, rows), row).start()

    @pl.loop(chunks - DELAY + HALF, chunks)
    def _(i):
        second_pass(i)

    def place(d, wide, first):
        j = delta + d

        @pl.when(jnp.logical_and(inside(j), j != col))
        def _():
            piece_copy(clamped(j), d, wide, first).wait_recv()

        @pl.when(inside(j))
        def _():
            for s in range(first, first + wide):
                at = pl.ds(pl.multiple_of((d + s - 1) * TOK, TOK), TOK)
                for t in range(TOK):
                    pair_out[clamped(j) * TOK + t, at] = piece_v[d + 1, t, s * TOK : (s + 1) * TOK]

    all_readers(place)

    @pl.loop(chunks - LAG, chunks)
    def _(i):
        finish(i)

    def sent_piece(cond, target, d, wide, first):
        @pl.when(jnp.logical_and(cond, target != col))
        def _():
            piece_copy(target, d, wide, first).wait_send()

    to_owners(sent_piece)
    all_readers(band_sent)

    @pl.loop(0, chunks)
    def _(i):
        @pl.when(has_next)
        def _():
            to_next(i).wait_send()
            grad_to_next(i).wait_send()

        @pl.when(has_prev)
        def _():
            to_prev(i).wait_send()
            grad_to_prev(i).wait_send()

    @pl.loop(1, cols)
    def _(d):
        a_copy(lax.rem(col + d, cols), col).wait_send()

    @pl.loop(1, rows)
    def _(d):
        source = lax.rem(row + d, rows)
        b_copy(source, source).wait_recv()

    total = red_b[0]
    for j in range(1, rows):
        total = total + red_b[j]
    wgrad_out[...] = total

    @pl.loop(1, rows)
    def _(d):
        b_copy(lax.rem(row + d, rows), row).wait_send()


def final_kernel(upd_in, grad_in, pair_in, wsum, upd_out, grad_out, pair_out, wgrad, sems):
    copies = [
        pltpu.make_async_copy(src, dst, sems.at[n])
        for n, (src, dst) in enumerate([(pair_in, pair_out), (upd_in, upd_out), (grad_in, grad_out)])
    ]
    for copy in copies:
        copy.start()
    wgrad[...] = wsum[:HEADS]
    for copy in copies:
        copy.wait()


def on_device(rows, cols, atom_rows, pair_rep, wqg, wkv, wo, pw, counts, token_mask, cotangent):
    samples = atom_rows.shape[0]
    chunks = samples // STEP
    vmem = pl.BlockSpec(memory_space=pltpu.VMEM)
    hbm = pl.BlockSpec(memory_space=pltpu.HBM)
    own = (samples, BLOCK, CH)
    halo = (samples, HALO, CH)
    dma = pltpu.SemaphoreType.DMA
    upd, grad, pair, wsum = pl.pallas_call(
        functools.partial(main_kernel, rows, cols, samples),
        out_shape=(
            jax.ShapeDtypeStruct(own, BF16),
            jax.ShapeDtypeStruct(own, BF16),
            jax.ShapeDtypeStruct(pair_rep.shape, BF16),
            jax.ShapeDtypeStruct((8, CH), F32),
        ),
        in_specs=[hbm] * 9,
        out_specs=(vmem,) * 4,
        scratch_shapes=[
            pltpu.SMEM((TOK, rows * cols), jnp.int32), pltpu.SMEM((rows * cols * TOK,), jnp.int32),
            pltpu.VMEM((CH, 2 * CH), BF16), pltpu.VMEM((CH, 2 * CH), BF16), pltpu.VMEM((CH, CH), BF16),
            pltpu.VMEM((HEADS, CH), F32), pltpu.VMEM((CH, 8), F32),
            pltpu.VMEM(own, BF16), pltpu.VMEM(own, BF16),
            pltpu.VMEM(halo, BF16), pltpu.VMEM(halo, BF16),
            pltpu.VMEM(halo, BF16), pltpu.VMEM(halo, BF16),
            pltpu.VMEM(halo, BF16), pltpu.VMEM(halo, BF16),
            pltpu.VMEM(own, F32),
            pltpu.VMEM((TOK, 3 * TOK, CH), BF16), pltpu.VMEM((TOK, 3 * TOK, CH), BF16),
            pltpu.VMEM((rows + 2, TOK, 3 * TOK, CH), BF16),
            pltpu.VMEM((2, KEYS, KEYS), F32), pltpu.VMEM((2, KEYS, KEYS), F32),
            pltpu.VMEM((samples, EXT, 2 * CH), BF16), pltpu.VMEM((STEP, EXT, 2 * CH), BF16),
            pltpu.VMEM(own, BF16), pltpu.VMEM((STEP, BLOCK, CH), F32),
            pltpu.VMEM((STEP, BLOCK, CH), BF16), pltpu.VMEM((STEP, BLOCK, CH), BF16),
            pltpu.VMEM(own, BF16), pltpu.VMEM((STEP, BLOCK, CH), BF16), pltpu.VMEM(own, BF16),
            pltpu.VMEM((samples, 2, KEYS, KEYS), BF16), pltpu.VMEM((samples, 2, KEYS, KEYS), BF16),
            pltpu.VMEM((STEP, EXT, LANES), F32), pltpu.VMEM((STEP, EXT, LANES), F32),
            pltpu.VMEM((cols, 8, CH), F32), pltpu.VMEM((rows, 8, CH), F32),
            pltpu.VMEM((8, CH), F32), pltpu.VMEM((8, CH), F32),
            dma((8,)),
            dma((chunks,)), dma((chunks,)), dma((chunks,)), dma((chunks,)),
            dma((chunks,)), dma((chunks,)), dma((chunks,)), dma((chunks,)),
            dma((rows + 2,)), dma((2,)), dma((2,)), dma((rows + 2,)),
            dma((cols,)), dma((cols,)), dma((rows,)), dma((rows,)),
        ],
        compiler_params=pltpu.CompilerParams(
            collective_id=0, has_side_effects=True, vmem_limit_bytes=40 * 2**20),
    )(*[
        pltpu.with_memory_space_constraint(array, pltpu.HBM)
        for array in (counts.T, token_mask, atom_rows, pair_rep, wqg, wkv, wo, pw.T, cotangent)
    ])
    upd, grad, pair_grad, wgrad = pl.pallas_call(
        final_kernel,
        out_shape=(
            jax.ShapeDtypeStruct(own, BF16),
            jax.ShapeDtypeStruct(own, BF16),
            jax.ShapeDtypeStruct(pair_rep.shape, BF16),
            jax.ShapeDtypeStruct((HEADS, CH), F32),
        ),
        in_specs=[vmem, vmem, vmem, vmem],
        out_specs=(hbm, hbm, hbm, vmem),
        scratch_shapes=[dma((3,))],
        compiler_params=pltpu.CompilerParams(vmem_limit_bytes=8 * 2**20),
    )(upd, grad, pair, wsum)
    return upd, grad, pair_grad, wgrad.T


def solution(mesh):
    rows, cols = mesh.shape["row"], mesh.shape["col"]
    atoms = P(None, ("row", "col"), None)
    pairs = P("row", "col", None)
    return jax.shard_map(
        functools.partial(on_device, rows, cols),
        mesh=mesh,
        in_specs=(atoms, pairs, P(), P(), P(), P(), P(), P(), atoms),
        out_specs=(atoms, atoms, pairs, P()),
        check_vma=False,
    )
```

profile of v0, /device:TPU:1, one launch (start us, length us, event | category | flops | bytes accessed | tf_op | source)
XLA Modules:
  0.0 54.6 jit_solution(15413297118978478182)
XLA Ops:
  0.6 51.5 %shard_map.120 = (bf16[48,64,128]{2,1,0:T(8,128)(2,1)S(1)}, bf16[48,64,128]{2,1,0:T(8,128)(2,1)S(1)}, bf16[128,64,128]{2,1,0:T(8,128)(2,1)S(1)}, f32[8,128]{1,0:T(8,128)S(1)}) custom-call(s32[8,128]{1,0:T(8,128)} %bitcast.3, s32[1024]{0:T(1024)} %mask_hbm.1, bf16[48,64,128]{2,1,0:T(8,128)(2,1)} %x_hbm.1, bf16[128,64,128]{2,1,0:T(8,128)(2,1)} %pair_hbm.1, ...), custom_call_target="tpu_custom_call" | custom-call | tf_op jit(solution)/shard_map/pallas_call | solution.py:620
  52.1 2.4 %shard_map.121 = (bf16[48,64,128]{2,1,0:T(8,128)(2,1)}, bf16[48,64,128]{2,1,0:T(8,128)(2,1)}, bf16[128,64,128]{2,1,0:T(8,128)(2,1)}, f32[4,128]{1,0:T(4,128)}) custom-call(bf16[48,64,128]{2,1,0:T(8,128)(2,1)S(1)} %get-tuple-element.12.upd_in, bf16[48,64,128]{2,1,0:T(8,128)(2,1)S(1)} %get-tuple-element.13.grad_in, ...), custom_call_target="tpu_custom_call" | custom-call | tf_op jit(solution)/shard_map/pallas_call | solution.py:662
where the time goes:
time: 54.7 us; the launch traced here: 54.6 us
  Pallas kernels  53.9 us (99%)
  between operations  0.64 us (1%)
    pallas_call x1, Pallas kernels, on_device(): pl.pallas_call(functools.partial(main_kernel, rows, cols, samples), out_s...  51.5 us
    pallas_call x1, Pallas kernels, on_device(): pl.pallas_call(final_kernel, out_shape=(jax.ShapeDtypeStruct(own, BF16),...  2.43 us

commit v1 on v0

--- a/solution.py
+++ b/solution.py
@@ -20,11 +20,11 @@
 EPS = 1e-05
 MASKED = -1000000000.0
 SCALE = 1.0 / math.sqrt(CH // HEADS)
-STEP = 4
+STEP = 8
 AHEAD = 3
-LAG = 4
-DELAY = 4
-HALF = 2
+LAG = 2
+DELAY = 1
+HALF = 1
 
 F32 = jnp.float32
 BF16 = jnp.bfloat16

time: 54.7 us -> 49.5 us (0.905)
  Pallas kernels: 53.9 us -> 48.7 us
    pallas_call x1, Pallas kernels: 51.5 us -> 46.2 us  [on_device(): pl.pallas_call(functools.partial(main_kernel, rows, cols, samples), out_s...]
where the time goes in v1:
time: 49.5 us; the launch traced here: 49.3 us
  Pallas kernels  48.7 us (98%)
  between operations  0.64 us (1%)
    pallas_call x1, Pallas kernels, on_device(): pl.pallas_call(functools.partial(main_kernel, rows, cols, samples), out_s...  46.2 us
    pallas_call x1, Pallas kernels, on_device(): pl.pallas_call(final_kernel, out_shape=(jax.ShapeDtypeStruct(own, BF16),...  2.43 us

profile of v1, /device:TPU:1, one launch (start us, length us, event | category | flops | bytes accessed | tf_op | source)
XLA Modules:
  0.0 49.3 jit_solution(5059882056773860129)
XLA Ops:
  0.6 46.2 %shard_map.120 = (bf16[48,64,128]{2,1,0:T(8,128)(2,1)S(1)}, bf16[48,64,128]{2,1,0:T(8,128)(2,1)S(1)}, bf16[128,64,128]{2,1,0:T(8,128)(2,1)S(1)}, f32[8,128]{1,0:T(8,128)S(1)}) custom-call(s32[8,128]{1,0:T(8,128)} %bitcast.3, s32[1024]{0:T(1024)} %mask_hbm.1, bf16[48,64,128]{2,1,0:T(8,128)(2,1)} %x_hbm.1, bf16[128,64,128]{2,1,0:T(8,128)(2,1)} %pair_hbm.1, ...), custom_call_target="tpu_custom_call" | custom-call | tf_op jit(solution)/shard_map/pallas_call | solution.py:620
  46.9 2.4 %shard_map.121 = (bf16[48,64,128]{2,1,0:T(8,128)(2,1)}, bf16[48,64,128]{2,1,0:T(8,128)(2,1)}, bf16[128,64,128]{2,1,0:T(8,128)(2,1)}, f32[4,128]{1,0:T(4,128)}) custom-call(bf16[48,64,128]{2,1,0:T(8,128)(2,1)S(1)} %get-tuple-element.12.upd_in, bf16[48,64,128]{2,1,0:T(8,128)(2,1)S(1)} %get-tuple-element.13.grad_in, ...), custom_call_target="tpu_custom_call" | custom-call | tf_op jit(solution)/shard_map/pallas_call | solution.py:662

commit v2 on v1

--- a/solution.py
+++ b/solution.py
@@ -22,7 +22,7 @@
 SCALE = 1.0 / math.sqrt(CH // HEADS)
 STEP = 8
 AHEAD = 3
-LAG = 2
+LAG = 4
 DELAY = 1
 HALF = 1
 

time: 49.5 us -> 49.1 us (level)
  Pallas kernels: 48.7 us -> 47.8 us
    pallas_call x1, Pallas kernels: 46.2 us -> 45.4 us  [on_device(): pl.pallas_call(functools.partial(main_kernel, rows, cols, samples), out_s...]
where the time goes in v2:
time: 49.1 us; the launch traced here: 48.5 us
  Pallas kernels  47.8 us (97%)
  between operations  0.64 us (1%)
    pallas_call x1, Pallas kernels, on_device(): pl.pallas_call(functools.partial(main_kernel, rows, cols, samples), out_s...  45.4 us
    pallas_call x1, Pallas kernels, on_device(): pl.pallas_call(final_kernel, out_shape=(jax.ShapeDtypeStruct(own, BF16),...  2.43 us

profile of v2, /device:TPU:1, one launch (start us, length us, event | category | flops | bytes accessed | tf_op | source)
XLA Modules:
  0.0 48.5 jit_solution(7792343479705747197)
XLA Ops:
  0.6 45.4 %shard_map.120 = (bf16[48,64,128]{2,1,0:T(8,128)(2,1)S(1)}, bf16[48,64,128]{2,1,0:T(8,128)(2,1)S(1)}, bf16[128,64,128]{2,1,0:T(8,128)(2,1)S(1)}, f32[8,128]{1,0:T(8,128)S(1)}) custom-call(s32[8,128]{1,0:T(8,128)} %bitcast.3, s32[1024]{0:T(1024)} %mask_hbm.1, bf16[48,64,128]{2,1,0:T(8,128)(2,1)} %x_hbm.1, bf16[128,64,128]{2,1,0:T(8,128)(2,1)} %pair_hbm.1, ...), custom_call_target="tpu_custom_call" | custom-call | tf_op jit(solution)/shard_map/pallas_call | solution.py:620
  46.0 2.4 %shard_map.121 = (bf16[48,64,128]{2,1,0:T(8,128)(2,1)}, bf16[48,64,128]{2,1,0:T(8,128)(2,1)}, bf16[128,64,128]{2,1,0:T(8,128)(2,1)}, f32[4,128]{1,0:T(4,128)}) custom-call(bf16[48,64,128]{2,1,0:T(8,128)(2,1)S(1)} %get-tuple-element.12.upd_in, bf16[48,64,128]{2,1,0:T(8,128)(2,1)S(1)} %get-tuple-element.13.grad_in, ...), custom_call_target="tpu_custom_call" | custom-call | tf_op jit(solution)/shard_map/pallas_call | solution.py:662

commit v3 on v2

--- a/solution.py
+++ b/solution.py
@@ -20,9 +20,9 @@
 EPS = 1e-05
 MASKED = -1000000000.0
 SCALE = 1.0 / math.sqrt(CH // HEADS)
-STEP = 8
-AHEAD = 3
-LAG = 4
+STEP = 12
+AHEAD = 2
+LAG = 3
 DELAY = 1
 HALF = 1
 

time: 49.1 us -> 49.2 us (level)
  no operation moved by 1% of the time
where the time goes in v3:
time: 49.2 us; the launch traced here: 48.7 us
  Pallas kernels  48.1 us (98%)
  between operations  0.64 us (1%)
    pallas_call x1, Pallas kernels, on_device(): pl.pallas_call(functools.partial(main_kernel, rows, cols, samples), out_s...  45.6 us
    pallas_call x1, Pallas kernels, on_device(): pl.pallas_call(final_kernel, out_shape=(jax.ShapeDtypeStruct(own, BF16),...  2.43 us

profile of v3, /device:TPU:1, one launch (start us, length us, event | category | flops | bytes accessed | tf_op | source)
XLA Modules:
  0.0 48.7 jit_solution(4219859657286283464)
XLA Ops:
  0.6 45.6 %shard_map.120 = (bf16[48,64,128]{2,1,0:T(8,128)(2,1)S(1)}, bf16[48,64,128]{2,1,0:T(8,128)(2,1)S(1)}, bf16[128,64,128]{2,1,0:T(8,128)(2,1)S(1)}, f32[8,128]{1,0:T(8,128)S(1)}) custom-call(s32[8,128]{1,0:T(8,128)} %bitcast.3, s32[1024]{0:T(1024)} %mask_hbm.1, bf16[48,64,128]{2,1,0:T(8,128)(2,1)} %x_hbm.1, bf16[128,64,128]{2,1,0:T(8,128)(2,1)} %pair_hbm.1, ...), custom_call_target="tpu_custom_call" | custom-call | tf_op jit(solution)/shard_map/pallas_call | solution.py:620
  46.3 2.4 %shard_map.121 = (bf16[48,64,128]{2,1,0:T(8,128)(2,1)}, bf16[48,64,128]{2,1,0:T(8,128)(2,1)}, bf16[128,64,128]{2,1,0:T(8,128)(2,1)}, f32[4,128]{1,0:T(4,128)}) custom-call(bf16[48,64,128]{2,1,0:T(8,128)(2,1)S(1)} %get-tuple-element.12.upd_in, bf16[48,64,128]{2,1,0:T(8,128)(2,1)S(1)} %get-tuple-element.13.grad_in, ...), custom_call_target="tpu_custom_call" | custom-call | tf_op jit(solution)/shard_map/pallas_call | solution.py:662
